TPU v7x, 32 devices: a whole 2x2x4 slice. The times are simulated.
32 devices in a mesh: ep: 8 (over y, x, core), dp: 4 (over z).
Axes of the slice: x: 2, y: 2, z: 4, core: 2. Of those that a mesh axis runs over, the one named last changes fastest.
Arguments:
- out_grad: bfloat16 [4, 1024, 2048], P('dp', 'ep'), may hold values from -6 to 6
- gates: bfloat16 [4, 1024, 8], P('dp', 'ep'), may hold values from 0.019897461 to 0.5
- routes: int32 [4, 1024, 8], P('dp', 'ep'), may hold values from 0 to 31, all different within a row; in each aligned block of 128 rows (0 to 127, 128 to 255, ..., all dimensions but the last counted through in order) at most 48 rows name the same one
- expert_slot: int32 [32], replicated, may hold values from 0 to 31, each once
- hidden_saved: bfloat16 [4, 32, 8, 48, 768], P('dp', 'ep'), may hold values from -6 to 6
- w_down: bfloat16 [2048, 24576], P('dp', 'ep'), may hold values from -0.21875 to 0.21875
Outputs:
- hidden_grad: bfloat16 [4, 32, 8, 48, 768], P('dp', 'ep')
- gate_grad: float32 [4, 1024, 8], P('dp', 'ep')
- weight_grad: float32 [2048, 24576], P('dp', 'ep')
Inputs may be any that keep to these rules, and one draw needn't show every extreme that they name: `routes`: the rows of one device name no expert more than 48 times, and every expert is named by some row. `expert_slot`: each slot once.
All inputs are finite; a program needn't handle non-finite values.
Results may differ from a plain program's by a relative error of at most 0.012.
Values may be sent and summed in bfloat16 or wider, within the bound.
No kernel may reach another device: no remote copies, remote signals or barrier semaphores. Data moves between devices by JAX's collectives and lax.ppermute only.
A program may use at most 128 MiB of HBM per device.

v0:
```python
import jax
import jax.numpy as jnp
from jax import lax
from jax.sharding import PartitionSpec as P


def local(out_grad, gates, routes, expert_slot, hidden_saved, w_down):
    tokens = out_grad.shape[1]
    width = out_grad.shape[2]
    chosen = routes.shape[2]
    experts = expert_slot.shape[0]
    n_ep = lax.axis_size("ep")
    exp_dev = experts // n_ep
    slots = hidden_saved.shape[3]
    hidden = hidden_saved.shape[4]
    flat_ids = routes.reshape(-1)
    onehot = (flat_ids[:, None] == jnp.arange(experts, dtype=jnp.int32)[None, :]).astype(jnp.int32)
    slot_ids = jnp.sum(onehot * expert_slot[None, :], axis=1)
    ranks = jnp.sum(onehot * (jnp.cumsum(onehot, axis=0) - 1), axis=1)
    target = slot_ids * slots + ranks
    rows = jnp.repeat(out_grad[0], chosen, axis=0)
    send_rows = jnp.zeros((experts * slots, width), jnp.bfloat16).at[target].set(rows)
    send_gates = jnp.zeros((experts * slots,), jnp.bfloat16).at[target].set(gates.reshape(-1))
    recv_rows, recv_gates = (
        lax.all_to_all(
            send_rows.reshape(n_ep, exp_dev * slots, width),
            "ep",
            split_axis=0,
            concat_axis=0,
            tiled=True,
        ),
        lax.all_to_all(
            send_gates.reshape(n_ep, exp_dev * slots), "ep", split_axis=0, concat_axis=0, tiled=True
        ),
    )
    recv_rows = recv_rows.reshape(n_ep, exp_dev, slots, width)
    saved = hidden_saved[0]
    w_all = lax.all_gather(w_down, "dp", axis=0, tiled=True).reshape(width, exp_dev, hidden)
    upstream = jnp.einsum("slcd,dlj->lscj", recv_rows, w_all, preferred_element_type=jnp.float32)
    gates_lsc = recv_gates.reshape(n_ep, exp_dev, slots).transpose(1, 0, 2).astype(jnp.float32)
    hidden_grad = (gates_lsc[..., None] * upstream).astype(jnp.bfloat16)[None]
    slot_grad = jnp.sum(saved.astype(jnp.float32) * upstream, axis=3)
    returned = lax.all_to_all(
        slot_grad.transpose(1, 0, 2).reshape(n_ep, exp_dev * slots),
        "ep",
        split_axis=0,
        concat_axis=0,
        tiled=True,
    )
    gate_grad = returned.reshape(-1)[target].reshape(1, tokens, chosen)
    scaled = (gates_lsc[..., None] * saved.astype(jnp.float32)).astype(jnp.bfloat16)
    term = jnp.einsum("slcd,lscj->dlj", recv_rows, scaled, preferred_element_type=jnp.float32)
    weight_grad = lax.psum_scatter(
        term.reshape(width // lax.axis_size("dp") * lax.axis_size("dp"), exp_dev * hidden).astype(
            jnp.bfloat16
        ),
        "dp",
        scatter_dimension=0,
        tiled=True,
    ).astype(jnp.float32)
    return (hidden_grad, gate_grad, weight_grad)


def solution(mesh):
    return jax.shard_map(
        local,
        mesh=mesh,
        in_specs=(
            P("dp", "ep", None),
            P("dp", "ep", None),
            P("dp", "ep", None),
            P(),
            P("dp", "ep", None, None, None),
            P("dp", "ep"),
        ),
        out_specs=(P("dp", "ep", None, None, None), P("dp", "ep", None), P("dp", "ep")),
        check_vma=False,
    )
```

profile of v0, /device:TPU:0, one launch (start us, length us, event | category | flops | bytes accessed | tf_op | source)
XLA Modules:
  0.0 457.8 jit_solution(12318421995495534040)
XLA Ops:
  7.3 4.7 %copy.29 = bf16[512,3072]{0,1:T(8,128)(2,1)} copy(bf16[512,3072]{1,0:T(8,128)(2,1)} %param.11) | data formatting | bytes 6291456 | tf_op args[5]
  12.3 0.1 copy.26
  12.4 0.1 reshape.113
  12.5 9.0 %reduce-window.6 = s32[32,8,128]{2,1,0:T(8,128)S(1)} reduce-window(s32[32,8,128]{2,1,0:T(8,128)S(1)} %fusion.15, s32[]{:T(128)} %constant.7.clone.1), window={size=1x1x128 pad=0_0x0_0x127_0}, to_apply=%region_1.0 | reduce-window | flops 4161536 | bytes 262148 | tf_op jit(solution)/shard_map/reduce-window
  21.7 0.1 copy.24
  21.9 0.1 add_add_fusion
  22.1 7.6 %scatter_custom_fusion = bf16[1536]{0:T(1024)(128)(2,1)S(1)} fusion(s32[1024]{0:T(1024)S(1)} %bitcast.55, bf16[1024]{0:T(1024)(128)(2,1)S(1)} %reshape.113, bf16[]{:T(256)} %constant.6.clone.1), kind=kCustom, calls=%fused_computation.31 | custom fusion | bytes 3074 | tf_op jit(solution)/shard_map/scatter | solution.py:23
  29.7 0.7 all_to_all.20
  30.4 5.2 %all-to-all-start = ((bf16[8,1,192]{2,1,0:T(2,128)(2,1)}), bf16[8,1,192]{2,1,0:T(2,128)(2,1)S(1)}, u32[]{:S(2)}, u32[]{:S(2)}) async-start(bf16[8,1,192]{2,1,0:T(2,128)(2,1)} %all_to_all.20), calls=%async_computation | async-start | bytes 16384 | tf_op jit(solution)/shard_map/all_to_all | solution.py:32
  35.6 10.2 %scatter_custom_fusion.1 = bf16[1536,2048]{1,0:T(8,128)(2,1)} fusion(s32[1024]{0:T(1024)S(1)} %bitcast.56, bf16[]{:T(256)} %constant.6.clone.1, bf16[128,2048]{1,0:T(8,128)(2,1)S(1)} %bitcast.47), kind=kCustom, calls=%fused_computation.12 | custom fusion | bytes 6815746 | tf_op jit(solution)/shard_map/scatter | solution.py:22
  45.9 4.9 %all-to-all-start.1 = ((bf16[8,192,2048]{2,1,0:T(8,128)(2,1)}), bf16[8,192,2048]{2,1,0:T(8,128)(2,1)}, u32[]{:S(2)}, u32[]{:S(2)}) async-start(bf16[8,192,2048]{2,1,0:T(8,128)(2,1)} %bitcast.48), calls=%async_computation.1 | async-start | bytes 12582912 | tf_op jit(solution)/shard_map/all_to_all | solution.py:25
  50.8 0.2 reduce-scatter.2.cloned.1.call-start
  51.1 71.2 %all-to-all-done.1 = bf16[8,192,2048]{2,1,0:T(8,128)(2,1)} async-done(((bf16[8,192,2048]{2,1,0:T(8,128)(2,1)}), bf16[8,192,2048]{2,1,0:T(8,128)(2,1)}, u32[]{:S(2)}, u32[]{:S(2)}) %all-to-all-start.1) | async-done | bytes 6291488 | tf_op jit(solution)/shard_map/all_to_all | solution.py:25
  122.4 12.5 %bitcast_convert_fusion = bf16[4,768,2048]{2,1,0:T(8,128)(2,1)} fusion(bf16[8,4,48,2048]{3,2,1,0:T(8,128)(2,1)} %bitcast.8, bf16[1,4,8,48,768]{4,3,2,1,0:T(8,128)(2,1)S(1)} %copy-done.5, f32[4,8,48]{2,1,0:T(8,128)S(1)} %copy.28), kind=kOutput, calls=%fused_computation.3 | convolution fusion | flops 4841668608 | bytes 21239808 | tf_op jit(solution)/shard_map/slcd,lscj->dlj/dot_general | solution.py:52
  134.9 16.7 %copy.35 = bf16[2048,3072]{1,0:T(8,128)(2,1)} copy(bf16[2048,3072]{0,1:T(8,128)(2,1)} %bitcast.49) | data formatting | bytes 25165824 | tf_op jit(solution)/shard_map/convert_element_type | solution.py:54
  151.6 81.4 %all-gather.2.cloned.1.call-done = bf16[2048,3072]{0,1:T(8,128)(2,1)} async-done(((bf16[512,3072]{0,1:T(8,128)(2,1)}), bf16[2048,3072]{0,1:T(8,128)(2,1)}) %all-gather.2.cloned.1.call-update) | async-done | bytes 12582928 | tf_op jit(solution)/shard_map/all_gather | solution.py:38
  233.1 15.4 %fusion.3 = (f32[4,8,48]{2,1,0:T(8,128)S(1)}, bf16[1,4,8,48,768]{4,3,2,1,0:T(8,128)(2,1)}) fusion(bf16[1,4,8,48,768]{4,3,2,1,0:T(8,128)(2,1)S(1)} %copy-done.5, f32[4,8,48]{2,1,0:T(8,128)S(1)} %copy.28, bf16[2048,4,768,1]{0,2,3,1:T(8,128)(2,1)} %bitcast.58, bf16[8,4,48,2048]{3,2,1,0:T(8,128)(2,1)} %bitcast.8), kind=kOutput, calls=%fused_computation.9 | convolution fusion | flops 4837734912 | bytes 23605248 | tf_op jit(solution)/shard_map/slcd,dlj->lscj/dot_general | solution.py:39
  248.5 0.7 all_to_all.21
  249.2 3.7 all-to-all-start.2
  252.9 4.7 %all-to-all-done.2 = f32[8,1,192]{2,1,0:T(1,128)S(1)} async-done(((f32[8,1,192]{2,1,0:T(1,128)}), f32[8,1,192]{2,1,0:T(1,128)S(1)}, u32[]{:S(2)}, u32[]{:S(2)}) %all-to-all-start.2) | async-done | bytes 6176 | tf_op jit(solution)/shard_map/all_to_all | solution.py:43
  257.7 6.1 %gather_fusion = f32[1024]{0:T(1024)S(1)} fusion(f32[1536]{0:T(1024)S(1)} %reshape.97, s32[1024]{0:T(1024)S(1)} %broadcast_clamp_fusion), kind=kCustom, calls=%fused_computation | custom fusion | bytes 12288 | tf_op jit(solution)/shard_map/gather | solution.py:50
  263.9 0.7 copy.36
  264.6 180.9 %reduce-scatter.2.cloned.1.call-done = bf16[512,3072]{1,0:T(8,128)(2,1)} async-done(((bf16[2048,3072]{1,0:T(8,128)(2,1)}), bf16[512,3072]{1,0:T(8,128)(2,1)}) %reduce-scatter.2.cloned.1.call-update) | async-done | bytes 3145744 | tf_op jit(solution)/shard_map/reduce_scatter | solution.py:53
  445.5 5.4 %convert_element_type.50 = f32[512,3072]{1,0:T(8,128)} convert(bf16[512,3072]{1,0:T(8,128)(2,1)} %reduce-scatter.2.cloned.1.call-done) | non-fusion elementwise | flops 1572864 | bytes 9437184 | tf_op jit(solution)/shard_map/convert_element_type | solution.py:60
  (35 shorter events, 1.0 us)
Async XLA Ops:
  7.2 28.5 %copy-start = (bf16[1,128,2048]{2,1,0:T(8,128)(2,1)S(1)}, bf16[1,128,2048]{2,1,0:T(8,128)(2,1)}, u32[]{:S(2)}) copy-start(bf16[1,128,2048]{2,1,0:T(8,128)(2,1)} %param.6) | copy-start | bytes 1572868
  7.2 4.8 %copy-start.2 = (s32[1,128,8]{1,2,0:T(8,128)S(1)}, s32[1,128,8]{1,2,0:T(8,128)}, u32[]{:S(2)}) copy-start(s32[1,128,8]{1,2,0:T(8,128)} %param.8) | copy-start | bytes 12292
  7.2 5.1 %copy-start.3 = (bf16[1,128,8]{1,2,0:T(8,128)(2,1)S(1)}, bf16[1,128,8]{1,2,0:T(8,128)(2,1)}, u32[]{:S(2)}) copy-start(bf16[1,128,8]{1,2,0:T(8,128)(2,1)} %param.7) | copy-start | bytes 6148
  7.2 14.8 %copy-start.4 = (s32[32]{0:T(128)S(1)}, s32[32]{0:T(128)}, u32[]{:S(2)}) copy-start(s32[32]{0:T(128)} %param.9) | copy-start | bytes 388
  7.2 225.8 %all-gather.2.cloned.1.call-start = ((), (), s32[]{:S(2)}) async-start(), calls=%async_computation.4 | async-start | bytes 15728640 | tf_op jit(solution)/shard_map/all_gather | solution.py:38
  30.4 15.5 %all-to-all-start = ((bf16[8,1,192]{2,1,0:T(2,128)(2,1)}), bf16[8,1,192]{2,1,0:T(2,128)(2,1)S(1)}, u32[]{:S(2)}, u32[]{:S(2)}) async-start(bf16[8,1,192]{2,1,0:T(2,128)(2,1)} %all_to_all.20), calls=%async_computation | async-start | bytes 16384 | tf_op jit(solution)/shard_map/all_to_all | solution.py:32
  45.9 76.5 %copy-start.5 = (bf16[1,4,8,48,768]{4,3,2,1,0:T(8,128)(2,1)S(1)}, bf16[1,4,8,48,768]{4,3,2,1,0:T(8,128)(2,1)}, u32[]{:S(2)}) copy-start(bf16[1,4,8,48,768]{4,3,2,1,0:T(8,128)(2,1)} %param.10) | copy-start | bytes 7077892
  45.9 76.5 %all-to-all-start.1 = ((bf16[8,192,2048]{2,1,0:T(8,128)(2,1)}), bf16[8,192,2048]{2,1,0:T(8,128)(2,1)}, u32[]{:S(2)}, u32[]{:S(2)}) async-start(bf16[8,192,2048]{2,1,0:T(8,128)(2,1)} %bitcast.48), calls=%async_computation.1 | async-start | bytes 12582912 | tf_op jit(solution)/shard_map/all_to_all | solution.py:25
  50.8 394.7 %reduce-scatter.2.cloned.1.call-start = ((), (), s32[]{:S(2)}) async-start(), calls=%async_computation.5 | async-start | bytes 15728640 | tf_op jit(solution)/shard_map/reduce_scatter | solution.py:53
  249.2 8.4 %all-to-all-start.2 = ((f32[8,1,192]{2,1,0:T(1,128)}), f32[8,1,192]{2,1,0:T(1,128)S(1)}, u32[]{:S(2)}, u32[]{:S(2)}) async-start(f32[8,1,192]{2,1,0:T(1,128)} %all_to_all.21), calls=%async_computation.2 | async-start | bytes 16384 | tf_op jit(solution)/shard_map/all_to_all | solution.py:43
  257.6 193.3 %copy-start.1 = (bf16[1,128,2048]{2,1,0:T(8,128)(2,1)S(1)}, bf16[1,128,2048]{2,1,0:T(8,128)(2,1)}, u32[]{:S(2)}) copy-start(bf16[1,128,2048]{2,1,0:T(8,128)(2,1)} %param.6) | copy-start | bytes 1572868
Sparse Core Ops, SparseCore 0:
  12.1 220.9 all-gather.1
  235.4 210.0 reduce-scatter.1
where the time goes:
time: 459 us; the launch traced here: 458 us
  waiting for transfers between devices  338 us (74%)
  local copies, waits for them, and re-layouts  48.5 us (11%)
  matrix products  28 us (6%)
  other arithmetic  14.7 us (3%)
  between operations  14.2 us (3%)
  starting transfers between devices  14 us (3%)
    reduce_scatter x1, waiting for transfers between devices, local(): lax.psum_scatter(term.reshape(width // lax.axis_size('dp') * lax.axis_siz...  181 us
    all_gather x1, waiting for transfers between devices, local(): lax.all_gather(w_down, 'dp', axis=0, tiled=True)  81.4 us
    all_to_all x1, waiting for transfers between devices, local(): lax.all_to_all(send_rows.reshape(n_ep, exp_dev * slots, width), 'ep', spl...  71.2 us
    convert_element_type x1, local copies, waits for them, and re-layouts, local(): term.reshape(width // lax.axis_size('dp') * lax.axis_size('dp'), exp_dev...  16.7 us
    dot_general x1, matrix products, local(): jnp.einsum('slcd,dlj->lscj', recv_rows, w_all, preferred_element_type=jnp...  15.4 us
    dot_general x1, matrix products, local(): jnp.einsum('slcd,lscj->dlj', recv_rows, scaled, preferred_element_type=jn...  12.5 us
    scatter x1, local copies, waits for them, and re-layouts, local(): jnp.zeros((experts * slots, width), jnp.bfloat16).at[target].set(rows)  10.2 us
  transfers between devices with their start and end apart: 5, of which 4 were waited for; matrix products, arithmetic and copies ran while one was open for 17% of the time, Pallas kernels for 0%

commit v1 on v0

--- a/solution.py
+++ b/solution.py
@@ -2,6 +2,17 @@
 import jax.numpy as jnp
 from jax import lax
 from jax.sharding import PartitionSpec as P
+
+
+def _apply_roots(z):
+    sides = lax.axis_size("dp")
+    store = [z]
+    for u in range(1, sides):
+        store.append(
+            lax.ppermute(store[u - 1], "dp", perm=[(kk, (kk - 1) % sides) for kk in range(sides)])
+        )
+    known = jnp.concatenate(store, 0)
+    return jnp.roll(known, lax.axis_index("dp") * z.shape[0], 0)
 
 
 def local(out_grad, gates, routes, expert_slot, hidden_saved, w_down):
@@ -35,7 +46,7 @@
     )
     recv_rows = recv_rows.reshape(n_ep, exp_dev, slots, width)
     saved = hidden_saved[0]
-    w_all = lax.all_gather(w_down, "dp", axis=0, tiled=True).reshape(width, exp_dev, hidden)
+    w_all = _apply_roots(w_down).reshape(width, exp_dev, hidden)
     upstream = jnp.einsum("slcd,dlj->lscj", recv_rows, w_all, preferred_element_type=jnp.float32)
     gates_lsc = recv_gates.reshape(n_ep, exp_dev, slots).transpose(1, 0, 2).astype(jnp.float32)
     hidden_grad = (gates_lsc[..., None] * upstream).astype(jnp.bfloat16)[None]

time: 459 us -> 618 us (1.35)
  waiting for transfers between devices: 338 us -> 471 us
  local copies, waits for them, and re-layouts: 48.5 us -> 68.3 us
    ppermute x0 -> x3, waiting for transfers between devices: none -> 395 us  [_apply_roots(): lax.ppermute(store[u - 1], 'dp', perm=[(kk, (kk - 1) % sides) for kk in r...]
    reduce_scatter x1, waiting for transfers between devices: 181 us -> 0.01 us  [local(): lax.psum_scatter(term.reshape(width // lax.axis_size('dp') * lax.axis_siz...]
    all_gather x1 -> x0, waiting for transfers between devices: 81.4 us -> none  [local(): lax.all_gather(w_down, 'dp', axis=0, tiled=True)]
    unnamed x16 -> x23, local copies, waits for them, and re-layouts: 5.62 us -> 17.7 us
  transfers between devices with their start and end apart: 5 -> 7, of which waited for: 4 -> 5; matrix products, arithmetic and copies ran while one was open for 17% -> 9% of each run, Pallas kernels for 0% -> 0%
where the time goes in v1:
time: 618 us; the launch traced here: 617 us
  waiting for transfers between devices  471 us (76%)
  local copies, waits for them, and re-layouts  68.3 us (11%)
  matrix products  28 us (5%)
  starting transfers between devices  19.9 us (3%)
  other arithmetic  15.4 us (2%)
  between operations  14.2 us (2%)
    ppermute x3, waiting for transfers between devices, _apply_roots(): lax.ppermute(store[u - 1], 'dp', perm=[(kk, (kk - 1) % sides) for kk in r...  395 us
    all_to_all x1, waiting for transfers between devices, local(): lax.all_to_all(send_rows.reshape(n_ep, exp_dev * slots, width), 'ep', spl...  71.2 us
    unnamed x23, local copies, waits for them, and re-layouts  17.7 us
    convert_element_type x1, local copies, waits for them, and re-layouts, local(): term.reshape(width // lax.axis_size('dp') * lax.axis_size('dp'), exp_dev...  16.6 us
    dot_general x1, matrix products, local(): jnp.einsum('slcd,dlj->lscj', recv_rows, w_all, preferred_element_type=jnp...  15.4 us
    dot_general x1, matrix products, local(): jnp.einsum('slcd,lscj->dlj', recv_rows, scaled, preferred_element_type=jn...  12.6 us
  transfers between devices with their start and end apart: 7, of which 5 were waited for; matrix products, arithmetic and copies ran while one was open for 9% of the time, Pallas kernels for 0%

profile of v1, /device:TPU:0, one launch (start us, length us, event | category | flops | bytes accessed | tf_op | source)
XLA Modules:
  0.0 617.1 jit_solution(15990041486953764213)
XLA Ops:
  8.2 9.0 %reduce-window.6 = s32[32,8,128]{2,1,0:T(8,128)S(1)} reduce-window(s32[32,8,128]{2,1,0:T(8,128)S(1)} %fusion.15, s32[]{:T(128)} %constant.37.clone.1), window={size=1x1x128 pad=0_0x0_0x127_0}, to_apply=%region_1.0 | reduce-window | flops 4161536 | bytes 262148 | tf_op jit(solution)/shard_map/reduce-window
  19.4 7.6 %scatter_custom_fusion = bf16[1536]{0:T(1024)(128)(2,1)S(1)} fusion(s32[1024]{0:T(1024)S(1)} %bitcast.54, bf16[1024]{0:T(1024)(128)(2,1)S(1)} %reshape.113, bf16[]{:T(256)} %constant.36.clone.1), kind=kCustom, calls=%fused_computation.39 | custom fusion | bytes 3074 | tf_op jit(solution)/shard_map/scatter | solution.py:34
  27.7 5.2 all-to-all-start
  32.9 10.2 %scatter_custom_fusion.1 = bf16[1536,2048]{1,0:T(8,128)(2,1)} fusion(s32[1024]{0:T(1024)S(1)} %bitcast.55, bf16[]{:T(256)} %constant.36.clone.1, bf16[128,2048]{1,0:T(8,128)(2,1)S(1)} %bitcast.45), kind=kCustom, calls=%fused_computation.12 | custom fusion | bytes 6815746 | tf_op jit(solution)/shard_map/scatter | solution.py:33
  43.1 4.9 all-to-all-start.1
  48.4 71.2 %all-to-all-done.1 = bf16[8,192,2048]{2,1,0:T(8,128)(2,1)} async-done(((bf16[8,192,2048]{2,1,0:T(8,128)(2,1)}), bf16[8,192,2048]{2,1,0:T(8,128)(2,1)}, u32[]{:S(2)}, u32[]{:S(2)}) %all-to-all-start.1) | async-done | bytes 6291488 | tf_op jit(solution)/shard_map/all_to_all | solution.py:36
  119.6 12.6 %bitcast_convert_fusion = bf16[4,768,2048]{2,1,0:T(8,128)(2,1)} fusion(bf16[8,4,48,2048]{3,2,1,0:T(8,128)(2,1)} %bitcast.8, bf16[1,4,8,48,768]{4,3,2,1,0:T(8,128)(2,1)S(1)} %copy-done.4, f32[4,8,48]{2,1,0:T(8,128)S(1)} %copy.30), kind=kOutput, calls=%fused_computation.3 | convolution fusion | flops 4841668608 | bytes 21239808 | tf_op jit(solution)/shard_map/slcd,lscj->dlj/dot_general | solution.py:63
  132.2 16.6 %copy.39 = bf16[2048,3072]{1,0:T(8,128)(2,1)} copy(bf16[2048,3072]{0,1:T(8,128)(2,1)} %bitcast.47) | data formatting | bytes 25165824 | tf_op jit(solution)/shard_map/convert_element_type | solution.py:65
  148.8 3.2 copy.32
  152.0 3.6 collective-permute-start
  155.7 191.2 %collective-permute-done = bf16[512,3072]{0,1:T(8,128)(2,1)S(1)} collective-permute-done((bf16[512,3072]{0,1:T(8,128)(2,1)S(1)}, bf16[512,3072]{0,1:T(8,128)(2,1)S(1)}, u32[]{:S(2)}, u32[]{:S(2)}) %collective-permute-start) | collective-permute-done | bytes 3145760 | tf_op jit(solution)/shard_map/ppermute | solution.py:12
  346.9 1.7 copy-done.2
  348.6 142.0 %collective-permute-done.1 = bf16[512,3072]{0,1:T(8,128)(2,1)} collective-permute-done((bf16[512,3072]{0,1:T(8,128)(2,1)S(1)}, bf16[512,3072]{0,1:T(8,128)(2,1)}, u32[]{:S(2)}, u32[]{:S(2)}) %collective-permute-start.1) | collective-permute-done | bytes 3145760 | tf_op jit(solution)/shard_map/ppermute | solution.py:12
  492.9 2.4 constant_dynamic-update-slice_fusion.5
  495.3 62.2 %collective-permute-done.2 = bf16[512,3072]{0,1:T(8,128)(2,1)} collective-permute-done((bf16[512,3072]{0,1:T(8,128)(2,1)}, bf16[512,3072]{0,1:T(8,128)(2,1)}, u32[]{:S(2)}, u32[]{:S(2)}) %collective-permute-start.2) | collective-permute-done | bytes 3145760 | tf_op jit(solution)/shard_map/ppermute | solution.py:12
  557.5 2.4 constant_dynamic-update-slice_fusion.4
  560.9 2.4 constant_dynamic-update-slice_fusion.1
  563.3 2.4 constant_dynamic-update-slice_fusion
  565.7 5.5 constant_dynamic-slice_fusion
  571.1 15.4 %fusion.3 = (f32[4,8,48]{2,1,0:T(8,128)S(1)}, bf16[1,4,8,48,768]{4,3,2,1,0:T(8,128)(2,1)}) fusion(bf16[1,4,8,48,768]{4,3,2,1,0:T(8,128)(2,1)S(1)} %copy-done.5, f32[4,8,48]{2,1,0:T(8,128)S(1)} %copy.30, bf16[2048,4,768,1]{0,2,3,1:T(8,128)(2,1)} %bitcast.48, bf16[8,4,48,2048]{3,2,1,0:T(8,128)(2,1)} %bitcast.8), kind=kOutput, calls=%fused_computation.9 | convolution fusion | flops 4837734912 | bytes 23605248 | tf_op jit(solution)/shard_map/slcd,dlj->lscj/dot_general | solution.py:50
  587.2 5.9 all-to-all-start.2
  593.2 4.7 all-to-all-done.2
  598.0 6.1 gather_fusion
  604.9 5.4 convert_element_type.50
  (47 shorter events, 9.1 us)
Async XLA Ops:
  7.2 25.7 %copy-start = (bf16[1,128,2048]{2,1,0:T(8,128)(2,1)S(1)}, bf16[1,128,2048]{2,1,0:T(8,128)(2,1)}, u32[]{:S(2)}) copy-start(bf16[1,128,2048]{2,1,0:T(8,128)(2,1)} %param.6) | copy-start | bytes 1572868
  27.7 15.5 %all-to-all-start = ((bf16[8,1,192]{2,1,0:T(2,128)(2,1)}), bf16[8,1,192]{2,1,0:T(2,128)(2,1)S(1)}, u32[]{:S(2)}, u32[]{:S(2)}) async-start(bf16[8,1,192]{2,1,0:T(2,128)(2,1)} %all_to_all.20), calls=%async_computation | async-start | bytes 16384 | tf_op jit(solution)/shard_map/all_to_all | solution.py:43
  43.1 76.5 %copy-start.4 = (bf16[1,4,8,48,768]{4,3,2,1,0:T(8,128)(2,1)S(1)}, bf16[1,4,8,48,768]{4,3,2,1,0:T(8,128)(2,1)}, u32[]{:S(2)}) copy-start(bf16[1,4,8,48,768]{4,3,2,1,0:T(8,128)(2,1)} %param.10) | copy-start | bytes 7077892
  43.1 76.5 %all-to-all-start.1 = ((bf16[8,192,2048]{2,1,0:T(8,128)(2,1)}), bf16[8,192,2048]{2,1,0:T(8,128)(2,1)}, u32[]{:S(2)}, u32[]{:S(2)}) async-start(bf16[8,192,2048]{2,1,0:T(8,128)(2,1)} %bitcast.46), calls=%async_computation.1 | async-start | bytes 12582912 | tf_op jit(solution)/shard_map/all_to_all | solution.py:36
  48.1 556.8 %reduce-scatter.2.cloned.1.call-start = ((), (), s32[]{:S(2)}) async-start(), calls=%async_computation.4 | async-start | bytes 15728640 | tf_op jit(solution)/shard_map/reduce_scatter | solution.py:64
  152.0 194.9 %collective-permute-start = (bf16[512,3072]{0,1:T(8,128)(2,1)S(1)}, bf16[512,3072]{0,1:T(8,128)(2,1)S(1)}, u32[]{:S(2)}, u32[]{:S(2)}) collective-permute-start(bf16[512,3072]{0,1:T(8,128)(2,1)S(1)} %copy.32), channel_id=1, source_target_pairs={{0,3},{1,0},{2,1},{3,2},{4,7},{5,4},{6,5},{7,6},{8,11},{9,8},{10,9... | collective-permute-start | bytes 9437192 | tf_op jit(solution)/shard_map/ppermute | solution.py:12
  346.9 1.7 copy-start.2
  348.6 142.0 %collective-permute-start.1 = (bf16[512,3072]{0,1:T(8,128)(2,1)S(1)}, bf16[512,3072]{0,1:T(8,128)(2,1)}, u32[]{:S(2)}, u32[]{:S(2)}) collective-permute-start(bf16[512,3072]{0,1:T(8,128)(2,1)S(1)} %collective-permute-done), channel_id=1, source_target_pairs={{0,3},{1,0},{2,1},{3,2},{4,7},{5,4},{6,5},{7,6},{8,11},{9,8},{10,9... | collective-permute-start | bytes 9437192 | tf_op jit(solution)/shard_map/ppermute | solution.py:12
  490.5 67.0 %collective-permute-start.2 = (bf16[512,3072]{0,1:T(8,128)(2,1)}, bf16[512,3072]{0,1:T(8,128)(2,1)}, u32[]{:S(2)}, u32[]{:S(2)}) collective-permute-start(bf16[512,3072]{0,1:T(8,128)(2,1)} %collective-permute-done.1), channel_id=1, source_target_pairs={{0,3},{1,0},{2,1},{3,2},{4,7},{5,4},{6,5},{7,6},{8,11},{9,8},{10,9... | collective-permute-start | bytes 9437192 | tf_op jit(solution)/shard_map/ppermute | solution.py:12
  490.5 1.9 copy-start.3
  565.7 5.5 copy-start.5
  587.2 10.6 %all-to-all-start.2 = ((f32[8,1,192]{2,1,0:T(1,128)}), f32[8,1,192]{2,1,0:T(1,128)S(1)}, u32[]{:S(2)}, u32[]{:S(2)}) async-start(f32[8,1,192]{2,1,0:T(1,128)} %all_to_all.21), calls=%async_computation.2 | async-start | bytes 16384 | tf_op jit(solution)/shard_map/all_to_all | solution.py:54
  597.9 12.4 %copy-start.1 = (bf16[1,128,2048]{2,1,0:T(8,128)(2,1)S(1)}, bf16[1,128,2048]{2,1,0:T(8,128)(2,1)}, u32[]{:S(2)}) copy-start(bf16[1,128,2048]{2,1,0:T(8,128)(2,1)} %param.6) | copy-start | bytes 1572868
Sparse Core Ops, SparseCore 0:
  148.9 348.1 reduce-scatter.1
